TPU v7x, 256 devices: a whole 4x4x8 slice. The times are simulated.
256 devices in a mesh: group: 2 (over z_lo), dp: 16 (over y, z_hi), mp: 8 (over x, core).
Axes of the slice: x: 4, y: 4, z: 8 (z_hi: 4, z_lo: 2; z = z_hi * 2 + z_lo), core: 2. Of those that a mesh axis runs over, the one named last changes fastest.
Arguments:
- teacher_hidden: bfloat16 [2048, 8192], P('dp', ('group', 'mp')), may hold values from -6 to 6
- teacher_gain: bfloat16 [8192], P(('group', 'mp')), may hold values from 0.25 to 1.75
- teacher_head: bfloat16 [8192, 8192], P(('group', 'mp')), may hold values from -0.198873782 to 0.198873782
- student_hidden: bfloat16 [2048, 4096], P('dp'), may hold values from -6 to 6
- student_head: bfloat16 [4096, 8192], P('dp', ('group', 'mp')), may hold values from -0.28125 to 0.28125
- depth_cut: int32 [32], P('dp'), may hold values from 1 to 4
Outputs:
- kl_terms: float32 [4, 2048], P(None, 'dp')
- hidden_grad: float32 [2048, 4096], P('dp', ('group', 'mp'))
- head_grad: float32 [4096, 8192], P('dp', ('group', 'mp'))
Inputs may be any that keep to these rules, and one draw needn't show every extreme that they name: `depth_cut`: each sample's number of codebooks kept.
All inputs are finite; a program needn't handle non-finite values.
Results may differ from a plain program's by a relative error of at most 0.0053.
Values may be sent and summed in bfloat16 or wider, within the bound.
No kernel may reach another device: no remote copies, remote signals or barrier semaphores. Data moves between devices by JAX's collectives and lax.ppermute only.
A program may use at most 128 MiB of HBM per device.

v0:
```python
import jax
import jax.numpy as jnp
from jax import lax
from jax.sharding import PartitionSpec as P

DT = 8192
C = 4
V = 2048
FRAMES = 64
epsilon = 1e-05


def from_everyone(value, axis):
    size = lax.axis_size(axis)
    return lax.all_to_all(
        jnp.broadcast_to(value[None], (size, *value.shape)), axis, 0, 0, tiled=True
    )


def of_everyone(value, axis):
    return from_everyone(value, axis).sum(axis=0)


def laid_out(parts, dim):
    parts = jnp.moveaxis(parts, 0, dim)
    shape = parts.shape
    return parts.reshape(*shape[:dim], shape[dim] * shape[dim + 1], *shape[dim + 2 :])


def gather_directly(value, axis, dim):
    return laid_out(from_everyone(value, axis), dim)


def in_blocks(value, dim, size):
    before, after = (value.shape[:dim], value.shape[dim + 1 :])
    return jnp.moveaxis(value.reshape(*before, size, -1, *after), dim, 0)


def sent_and_summed(value, axis, dim):
    size = lax.axis_size(axis)
    parts = lax.all_to_all(in_blocks(value, dim, size), axis, 0, 0, tiled=True)
    return jnp.sum(parts, axis=0)


def shards(teacher_hidden, teacher_gain, teacher_head, student_hidden, student_head, depth_cut):
    part_count = lax.axis_size(("group", "mp"))
    device_index = lax.axis_index(("group", "mp"))
    frame_count = teacher_hidden.shape[0]
    hidden_float = teacher_hidden.astype(jnp.float32)
    squares = of_everyone(jnp.sum(hidden_float * hidden_float, axis=1), ("group", "mp"))
    row_scale = lax.rsqrt(squares / DT + epsilon)
    normed = (hidden_float * row_scale[:, None] * teacher_gain.astype(jnp.float32)[None, :]).astype(
        jnp.bfloat16
    )
    student_full = lax.all_gather(student_head, "dp", axis=0, tiled=True)
    depth_rows = jnp.repeat(depth_cut, FRAMES)
    book_range = jnp.arange(C, dtype=jnp.int32)
    alive_mask = (book_range[None, :] < depth_rows[:, None]).astype(jnp.float32)
    depth_weight = alive_mask / depth_rows[:, None].astype(jnp.float32)
    row_total = frame_count // part_count
    sliced = normed
    teacher_rows = lax.psum_scatter(
        jnp.dot(sliced, teacher_head, preferred_element_type=jnp.float32),
        ("group", "mp"),
        scatter_dimension=0,
        tiled=True,
    )
    student_part = jnp.dot(student_hidden, student_full, preferred_element_type=jnp.float32)
    student_rows = lax.all_to_all(
        student_part, ("group", "mp"), split_axis=0, concat_axis=1, tiled=True
    )
    teacher_log = jax.nn.log_softmax(teacher_rows.reshape(row_total, C, V), axis=2)
    student_log = jax.nn.log_softmax(student_rows.reshape(row_total, C, V), axis=2)
    teacher_prob = jnp.exp(teacher_log)
    divergence = jnp.sum(teacher_prob * (teacher_log - student_log), axis=2)
    weight_rows = lax.dynamic_slice_in_dim(depth_weight, device_index * row_total, row_total, 0)
    kl_terms = gather_directly((divergence * weight_rows).T, ("group", "mp"), 1)
    grad_rows = (
        ((jnp.exp(student_log) - teacher_prob) * weight_rows[:, :, None])
        .reshape(row_total, C * V)
        .astype(jnp.bfloat16)
    )
    score_grad = lax.all_to_all(grad_rows, ("group", "mp"), split_axis=1, concat_axis=0, tiled=True)
    hidden_term = lax.dot_general(
        score_grad, student_full, (((1,), (1,)), ((), ())), preferred_element_type=jnp.float32
    )
    head_dims = (((0,), (0,)), ((), ()))
    hidden_grad = sent_and_summed(hidden_term, ("group", "mp"), 1)
    sliced = student_hidden
    head_grad = lax.psum_scatter(
        lax.dot_general(sliced, score_grad, head_dims, preferred_element_type=jnp.float32),
        "dp",
        scatter_dimension=0,
        tiled=True,
    )
    return (kl_terms, hidden_grad, head_grad)


def solution(mesh):
    return jax.shard_map(
        shards,
        mesh=mesh,
        in_specs=(
            P("dp", ("group", "mp")),
            P(("group", "mp")),
            P(("group", "mp"), None),
            P("dp", None),
            P("dp", ("group", "mp")),
            P("dp"),
        ),
        out_specs=(P(None, "dp"), P("dp", ("group", "mp")), P("dp", ("group", "mp"))),
        check_vma=False,
    )
```

profile of v0, /device:TPU:2, one launch (start us, length us, event | category | flops | bytes accessed | tf_op | source)
XLA Modules:
  0.0 294.2 jit_solution(6305861253287781479)
XLA Ops:
  8.1 0.7 all-gather.2.cloned.1.call-update
  8.7 1.0 fusion.10
  10.4 6.2 %all-to-all-start = ((f32[16,1,128]{2,1,0:T(1,128)}), f32[16,1,128]{2,1,0:T(1,128)S(1)}, u32[]{:S(2)}, u32[]{:S(2)}) async-start(f32[16,1,128]{2,1,0:T(1,128)} %broadcast_in_dim.6), calls=%async_computation | async-start | bytes 16384 | tf_op jit(solution)/shard_map/all_to_all | solution.py:15
  16.6 0.7 convert_element_type.28
  17.3 3.9 %all-to-all-done = f32[16,1,128]{2,1,0:T(1,128)S(1)} async-done(((f32[16,1,128]{2,1,0:T(1,128)}), f32[16,1,128]{2,1,0:T(1,128)S(1)}, u32[]{:S(2)}, u32[]{:S(2)}) %all-to-all-start) | async-done | bytes 8224 | tf_op jit(solution)/shard_map/all_to_all | solution.py:15
  21.2 6.7 %fusion.15 = f32[128,8192]{1,0:T(8,128)} fusion(bf16[512,8192]{1,0:T(8,128)(2,1)} %param.9, bf16[128,512]{1,0:T(8,128)(2,1)} %param.7, f32[512]{0:T(512)S(1)} %convert_element_type.28, f32[128]{0:T(128)S(1)} %add_rsqrt_fusion), kind=kOutput, calls=%fused_computation.24 | convolution fusion | flops 1074003968 | bytes 12716544 | tf_op jit(solution)/shard_map/dot_general | solution.py:63
  28.0 61.3 %all-gather.2.cloned.1.call-done = bf16[4096,512]{1,0:T(8,128)(2,1)} async-done(((bf16[256,512]{1,0:T(8,128)(2,1)}), bf16[4096,512]{1,0:T(8,128)(2,1)}) %all-gather.2.cloned.1.call-update) | async-done | bytes 4194320 | tf_op jit(solution)/shard_map/all_gather | solution.py:55
  89.3 3.6 %convolution_bitcast_fusion.2 = f32[16,8,512]{2,1,0:T(8,128)} fusion(bf16[128,4096]{1,0:T(8,128)(2,1)S(1)} %copy-done, bf16[4096,512]{1,0:T(8,128)(2,1)} %all-gather.2.cloned.1.call-done), kind=kOutput, calls=%fused_computation.12 | convolution fusion | flops 536870912 | bytes 5505024 | tf_op jit(solution)/shard_map/dot_general | solution.py:68
  93.0 11.4 %all-to-all-start.1 = ((f32[16,8,512]{2,1,0:T(8,128)}), f32[16,8,512]{2,1,0:T(8,128)S(1)}, u32[]{:S(2)}, u32[]{:S(2)}) async-start(f32[16,8,512]{2,1,0:T(8,128)} %convolution_bitcast_fusion.2), calls=%async_computation.2 | async-start | bytes 524288 | tf_op jit(solution)/shard_map/all_to_all | solution.py:69
  104.6 5.7 %all-to-all-done.1 = f32[16,8,512]{2,1,0:T(8,128)S(1)} async-done(((f32[16,8,512]{2,1,0:T(8,128)}), f32[16,8,512]{2,1,0:T(8,128)S(1)}, u32[]{:S(2)}, u32[]{:S(2)}) %all-to-all-start.1) | async-done | bytes 262176 | tf_op jit(solution)/shard_map/all_to_all | solution.py:69
  111.1 15.1 %reduce-scatter.3.cloned.1.call-done = f32[8,8192]{1,0:T(8,128)} async-done(((f32[128,8192]{1,0:T(8,128)}), f32[8,8192]{1,0:T(8,128)}) %reduce-scatter.3.cloned.1.call-update) | async-done | bytes 262160 | tf_op jit(solution)/shard_map/reduce_scatter | solution.py:62
  126.2 1.1 fusion.4
  127.3 0.9 multiply_reduce_fusion
  128.4 12.0 %all_to_all.48 = bf16[8,16,512]{2,0,1:T(8,128)(2,1)S(1)} all-to-all(bf16[8,16,512]{2,0,1:T(8,128)(2,1)S(1)} %bitcast.34), channel_id=1, replica_groups=mesh['group'=2,'dp'=16,'mp'=8] {'group','mp'}, dimensions={1} | all-to-all | bytes 262144 | tf_op jit(solution)/shard_map/all_to_all | solution.py:83
  140.4 4.5 %convolution_bitcast_fusion = f32[4096,512]{0,1:T(8,128)} fusion(bf16[128,4096]{1,0:T(8,128)(2,1)S(1)} %copy-done, bf16[8,16,512]{2,0,1:T(8,128)(2,1)S(1)} %all_to_all.48), kind=kOutput, calls=%fused_computation.4 | convolution fusion | flops 536870912 | bytes 9568256 | tf_op jit(solution)/shard_map/dot_general | solution.py:91
  144.9 0.6 broadcast_in_dim.8
  145.5 5.2 %all-to-all-start.2 = ((f32[16,4,8]{2,1,0:T(4,128)}), f32[16,4,8]{2,1,0:T(4,128)S(1)}, u32[]{:S(2)}, u32[]{:S(2)}) async-start(f32[16,4,8]{2,1,0:T(4,128)} %broadcast_in_dim.8), calls=%async_computation.3 | async-start | bytes 65536 | tf_op jit(solution)/shard_map/all_to_all | solution.py:15
  150.7 5.0 %convolution_bitcast_fusion.1 = f32[16,128,256]{2,1,0:T(8,128)} fusion(bf16[16,256,512]{2,1,0:T(8,128)(2,1)} %bitcast.32, bf16[8,16,512]{2,0,1:T(8,128)(2,1)S(1)} %all_to_all.48), kind=kOutput, calls=%fused_computation.11 | convolution fusion | flops 536870912 | bytes 6422528 | tf_op jit(solution)/shard_map/dot_general | solution.py:84
  155.7 5.8 %all-to-all-start.4 = ((f32[16,128,256]{2,1,0:T(8,128)}), f32[16,128,256]{2,1,0:T(8,128)S(1)}, u32[]{:S(2)}, u32[]{:S(2)}) async-start(f32[16,128,256]{2,1,0:T(8,128)} %convolution_bitcast_fusion.1), calls=%async_computation.5 | async-start | bytes 4194304 | tf_op jit(solution)/shard_map/all_to_all | solution.py:41
  161.5 0.7 reshape.56
  162.2 67.3 %all-to-all-done.4 = f32[16,128,256]{2,1,0:T(8,128)S(1)} async-done(((f32[16,128,256]{2,1,0:T(8,128)}), f32[16,128,256]{2,1,0:T(8,128)S(1)}, u32[]{:S(2)}, u32[]{:S(2)}) %all-to-all-start.4) | async-done | bytes 2097184 | tf_op jit(solution)/shard_map/all_to_all | solution.py:41
  229.5 0.8 reduce_sum.48
  230.3 54.4 %reduce-scatter.5.cloned.1.call-done = f32[256,512]{0,1:T(8,128)} async-done(((f32[4096,512]{0,1:T(8,128)}), f32[256,512]{0,1:T(8,128)}) %reduce-scatter.5.cloned.1.call-update) | async-done | bytes 524304 | tf_op jit(solution)/shard_map/reduce_scatter | solution.py:90
  284.7 2.0 copy.17
  (22 shorter events, 2.0 us)
Async XLA Ops:
  8.0 81.3 %copy-start = (bf16[128,4096]{1,0:T(8,128)(2,1)S(1)}, bf16[128,4096]{1,0:T(8,128)(2,1)}, u32[]{:S(2)}) copy-start(bf16[128,4096]{1,0:T(8,128)(2,1)} %param.10) | copy-start | bytes 3145732
  8.0 81.3 %all-gather.2.cloned.1.call-start = ((), (), s32[]{:S(2)}) async-start(), calls=%async_computation.8 | async-start | bytes 4456448 | tf_op jit(solution)/shard_map/all_gather | solution.py:55
  10.4 10.8 %all-to-all-start = ((f32[16,1,128]{2,1,0:T(1,128)}), f32[16,1,128]{2,1,0:T(1,128)S(1)}, u32[]{:S(2)}, u32[]{:S(2)}) async-start(f32[16,1,128]{2,1,0:T(1,128)} %broadcast_in_dim.6), calls=%async_computation | async-start | bytes 16384 | tf_op jit(solution)/shard_map/all_to_all | solution.py:15
  16.6 109.6 %reduce-scatter.3.cloned.1.call-start = ((), (), s32[]{:S(2)}) async-start(), calls=%async_computation.7 | async-start | bytes 4456448 | tf_op jit(solution)/shard_map/reduce_scatter | solution.py:62
  27.9 76.5 %copy-start.1 = (s32[2]{0:T(128)S(1)}, s32[2]{0:T(128)}, u32[]{:S(2)}) copy-start(s32[2]{0:T(128)} %param.12) | copy-start | bytes 28
  93.0 17.4 %all-to-all-start.1 = ((f32[16,8,512]{2,1,0:T(8,128)}), f32[16,8,512]{2,1,0:T(8,128)S(1)}, u32[]{:S(2)}, u32[]{:S(2)}) async-start(f32[16,8,512]{2,1,0:T(8,128)} %convolution_bitcast_fusion.2), calls=%async_computation.2 | async-start | bytes 524288 | tf_op jit(solution)/shard_map/all_to_all | solution.py:69
  104.4 180.3 %reduce-scatter.5.cloned.1.call-start = ((), (), s32[]{:S(2)}) async-start(), calls=%async_computation.9 | async-start | bytes 8912896 | tf_op jit(solution)/shard_map/reduce_scatter | solution.py:90
  145.5 10.2 %all-to-all-start.2 = ((f32[16,4,8]{2,1,0:T(4,128)}), f32[16,4,8]{2,1,0:T(4,128)S(1)}, u32[]{:S(2)}, u32[]{:S(2)}) async-start(f32[16,4,8]{2,1,0:T(4,128)} %broadcast_in_dim.8), calls=%async_computation.3 | async-start | bytes 65536 | tf_op jit(solution)/shard_map/all_to_all | solution.py:15
  155.7 73.8 %all-to-all-start.4 = ((f32[16,128,256]{2,1,0:T(8,128)}), f32[16,128,256]{2,1,0:T(8,128)S(1)}, u32[]{:S(2)}, u32[]{:S(2)}) async-start(f32[16,128,256]{2,1,0:T(8,128)} %convolution_bitcast_fusion.1), calls=%async_computation.5 | async-start | bytes 4194304 | tf_op jit(solution)/shard_map/all_to_all | solution.py:41
Sparse Core Ops, SparseCore 0:
  11.3 78.0 all-gather.1
  145.0 139.6 reduce-scatter.4
Sparse Core Ops, SparseCore 1:
  28.1 98.1 reduce-scatter.2
where the time goes:
time: 295 us; the launch traced here: 294 us
  waiting for transfers between devices  208 us (71%)
  starting transfers between devices  28.7 us (10%)
  matrix products  19.9 us (7%)
  between operations  15.5 us (5%)
  blocking collectives  12 us (4%)
  other arithmetic  5.51 us (2%)
  local copies, waits for them, and re-layouts  4.11 us (1%)
    all_to_all x1, waiting for transfers between devices, sent_and_summed(): parts = lax.all_to_all(in_blocks(value, dim, size), axis, 0, 0, tiled=True)  67.3 us
    all_gather x1, waiting for transfers between devices, shards(): student_full = lax.all_gather(student_head, 'dp', axis=0, tiled=True)  61.3 us
    reduce_scatter x1, waiting for transfers between devices, shards(): lax.psum_scatter(lax.dot_general(sliced, score_grad, head_dims, preferred...  54.4 us
    reduce_scatter x1, waiting for transfers between devices, shards(): lax.psum_scatter(jnp.dot(sliced, teacher_head, preferred_element_type=jnp...  15.1 us
    all_to_all x1, blocking collectives, shards(): lax.all_to_all(grad_rows, ('group', 'mp'), split_axis=1, concat_axis=0, t...  12 us
    all_to_all x1, starting transfers between devices, shards(): lax.all_to_all(student_part, ('group', 'mp'), split_axis=0, concat_axis=1...  11.4 us
    all_to_all x2, starting transfers between devices, from_everyone(): lax.all_to_all(jnp.broadcast_to(value[None], (size, *value.shape)), axis,...  11.4 us
    dot_general x1, matrix products, shards(): jnp.dot(sliced, teacher_head, preferred_element_type=jnp.float32)  6.7 us
  transfers between devices with their start and end apart: 7, of which 6 were waited for; matrix products, arithmetic and copies ran while one was open for 7% of the time, Pallas kernels for 0%

commit v1 on v0

--- a/solution.py
+++ b/solution.py
@@ -52,7 +52,10 @@
     normed = (hidden_float * row_scale[:, None] * teacher_gain.astype(jnp.float32)[None, :]).astype(
         jnp.bfloat16
     )
-    student_full = lax.all_gather(student_head, "dp", axis=0, tiled=True)
+    outer = lax.axis_size("dp")
+    extra = jnp.stack(outer * [student_head], axis=0)
+    back = lax.all_to_all(extra, "dp", 0, 0)
+    student_full = jnp.concatenate(back, axis=0)
     depth_rows = jnp.repeat(depth_cut, FRAMES)
     book_range = jnp.arange(C, dtype=jnp.int32)
     alive_mask = (book_range[None, :] < depth_rows[:, None]).astype(jnp.float32)

time: 295 us -> 323 us (1.095)
  waiting for transfers between devices: 208 us -> 219 us
  blocking collectives: 12 us -> 20.8 us
  starting transfers between devices: 28.7 us -> 36.5 us
    all_to_all x0 -> x1, waiting for transfers between devices: none -> 96.3 us  [shards(): back = lax.all_to_all(extra, 'dp', 0, 0)]
    all_gather x1 -> x0, waiting for transfers between devices: 61.3 us -> none  [shards(): student_full = lax.all_gather(student_head, 'dp', axis=0, tiled=True)]
    reduce_scatter x1, waiting for transfers between devices: 15.1 us -> 0.01 us  [shards(): lax.psum_scatter(jnp.dot(sliced, teacher_head, preferred_element_type=jnp...]
    all_to_all x0 -> x1, blocking collectives: none -> 10.7 us  [from_everyone(): lax.all_to_all(jnp.broadcast_to(value[None], (size, *value.shape)), axis,...]
    all_to_all x0 -> x1, starting transfers between devices: none -> 10.5 us  [shards(): back = lax.all_to_all(extra, 'dp', 0, 0)]
    all_to_all x2 -> x1, starting transfers between devices: 11.4 us -> 5.19 us  [from_everyone(): lax.all_to_all(jnp.broadcast_to(value[None], (size, *value.shape)), axis,...]
    reduce_scatter x1, waiting for transfers between devices: 54.4 us -> 50 us  [shards(): lax.psum_scatter(lax.dot_general(sliced, score_grad, head_dims, preferred...]
    all_to_all x2 -> x1, waiting for transfers between devices: 3.91 us -> 0.01 us  [from_everyone(): lax.all_to_all(jnp.broadcast_to(value[None], (size, *value.shape)), axis,...]
  transfers between devices with their start and end apart: 7 -> 6, of which waited for: 6 -> 4; matrix products, arithmetic and copies ran while one was open for 7% -> 6% of each run, Pallas kernels for 0% -> 0%
where the time goes in v1:
time: 323 us; the launch traced here: 322 us
  waiting for transfers between devices  219 us (68%)
  starting transfers between devices  36.5 us (11%)
  blocking collectives  20.8 us (6%)
  matrix products  20.2 us (6%)
  between operations  14.1 us (4%)
  local copies, waits for them, and re-layouts  6.79 us (2%)
  other arithmetic  4.93 us (2%)
    all_to_all x1, waiting for transfers between devices, shards(): back = lax.all_to_all(extra, 'dp', 0, 0)  96.3 us
    all_to_all x1, waiting for transfers between devices, sent_and_summed(): parts = lax.all_to_all(in_blocks(value, dim, size), axis, 0, 0, tiled=True)  67.5 us
    reduce_scatter x1, waiting for transfers between devices, shards(): lax.psum_scatter(lax.dot_general(sliced, score_grad, head_dims, preferred...  50 us
    all_to_all x1, starting transfers between devices, shards(): lax.all_to_all(student_part, ('group', 'mp'), split_axis=0, concat_axis=1...  14.9 us
    all_to_all x1, blocking collectives, from_everyone(): lax.all_to_all(jnp.broadcast_to(value[None], (size, *value.shape)), axis,...  10.7 us
    all_to_all x1, starting transfers between devices, shards(): back = lax.all_to_all(extra, 'dp', 0, 0)  10.5 us
    all_to_all x1, blocking collectives, shards(): lax.all_to_all(grad_rows, ('group', 'mp'), split_axis=1, concat_axis=0, t...  10.1 us
    dot_general x1, matrix products, shards(): jnp.dot(sliced, teacher_head, preferred_element_type=jnp.float32)  6.67 us
  transfers between devices with their start and end apart: 6, of which 4 were waited for; matrix products, arithmetic and copies ran while one was open for 6% of the time, Pallas kernels for 0%

profile of v1, /device:TPU:2, one launch (start us, length us, event | category | flops | bytes accessed | tf_op | source)
XLA Modules:
  0.0 322.4 jit_solution(13203745470821882301)
XLA Ops:
  7.2 1.1 fusion.12
  8.3 10.7 %all_to_all.50 = f32[16,1,128]{2,1,0:T(1,128)S(1)} all-to-all(f32[16,1,128]{2,1,0:T(1,128)S(1)} %broadcast_in_dim.6), channel_id=1, replica_groups=mesh['group'=2,'dp'=16,'mp'=8] {'group','mp'}, dimensions={0} | all-to-all | bytes 16384 | tf_op jit(solution)/shard_map/all_to_all | solution.py:15
  19.0 3.3 %stack.2 = bf16[16,256,512]{2,1,0:T(8,128)(2,1)} broadcast(bf16[256,512]{1,0:T(8,128)(2,1)} %param.11), dimensions={1,2} | broadcast | bytes 4456448 | tf_op jit(solution)/shard_map/stack | solution.py:56
  22.3 10.5 %all-to-all-start.1 = ((bf16[16,256,512]{2,1,0:T(8,128)(2,1)}), bf16[16,256,512]{2,1,0:T(8,128)(2,1)}, u32[]{:S(2)}, u32[]{:S(2)}) async-start(bf16[16,256,512]{2,1,0:T(8,128)(2,1)} %stack.2), calls=%async_computation.2 | async-start | bytes 8388608 | tf_op jit(solution)/shard_map/all_to_all | solution.py:57
  32.9 6.7 %fusion.17 = f32[128,8192]{1,0:T(8,128)} fusion(bf16[512,8192]{1,0:T(8,128)(2,1)} %param.9, bf16[128,512]{1,0:T(8,128)(2,1)S(1)} %copy-done.1, f32[512]{0:T(512)S(1)} %convert_element_type.28, f32[128]{0:T(128)S(1)} %add_rsqrt_fusion), kind=kOutput, calls=%fused_computation.25 | convolution fusion | flops 1074003968 | bytes 12716544 | tf_op jit(solution)/shard_map/dot_general | solution.py:66
  39.6 96.3 %all-to-all-done.1 = bf16[16,256,512]{2,1,0:T(8,128)(2,1)} async-done(((bf16[16,256,512]{2,1,0:T(8,128)(2,1)}), bf16[16,256,512]{2,1,0:T(8,128)(2,1)}, u32[]{:S(2)}, u32[]{:S(2)}) %all-to-all-start.1) | async-done | bytes 4194336 | tf_op jit(solution)/shard_map/all_to_all | solution.py:57
  135.9 3.6 %fusion.10 = f32[16,8,512]{2,1,0:T(8,128)} fusion(bf16[4096,512,1]{1,0,2:T(8,128)(2,1)} %bitcast.4, bf16[128,4096]{1,0:T(8,128)(2,1)S(1)} %copy-done), kind=kOutput, calls=%fused_computation.12 | convolution fusion | flops 536870912 | bytes 5505024 | tf_op jit(solution)/shard_map/dot_general | solution.py:71
  139.5 14.9 %all-to-all-start.2 = ((f32[16,8,512]{2,1,0:T(8,128)}), f32[16,8,512]{2,1,0:T(8,128)S(1)}, u32[]{:S(2)}, u32[]{:S(2)}) async-start(f32[16,8,512]{2,1,0:T(8,128)} %fusion.10), calls=%async_computation.3 | async-start | bytes 524288 | tf_op jit(solution)/shard_map/all_to_all | solution.py:72
  154.7 5.2 %all-to-all-done.2 = f32[16,8,512]{2,1,0:T(8,128)S(1)} async-done(((f32[16,8,512]{2,1,0:T(8,128)}), f32[16,8,512]{2,1,0:T(8,128)S(1)}, u32[]{:S(2)}, u32[]{:S(2)}) %all-to-all-start.2) | async-done | bytes 262176 | tf_op jit(solution)/shard_map/all_to_all | solution.py:72
  159.9 0.4 fusion.5
  160.3 0.4 fusion.8
  160.8 1.1 fusion.4
  161.9 0.9 multiply_reduce_fusion
  163.0 10.1 %all_to_all.51 = bf16[8,16,512]{2,0,1:T(8,128)(2,1)S(1)} all-to-all(bf16[8,16,512]{2,0,1:T(8,128)(2,1)S(1)} %bitcast.35), channel_id=1, replica_groups=mesh['group'=2,'dp'=16,'mp'=8] {'group','mp'}, dimensions={1} | all-to-all | bytes 262144 | tf_op jit(solution)/shard_map/all_to_all | solution.py:86
  173.1 4.5 %convolution_bitcast_fusion = f32[4096,512]{0,1:T(8,128)} fusion(bf16[128,4096]{1,0:T(8,128)(2,1)S(1)} %copy-done, bf16[8,16,512]{2,0,1:T(8,128)(2,1)S(1)} %all_to_all.51), kind=kOutput, calls=%fused_computation.4 | convolution fusion | flops 536870912 | bytes 9568256 | tf_op jit(solution)/shard_map/dot_general | solution.py:94
  177.6 0.6 broadcast_in_dim.8
  178.2 5.2 %all-to-all-start.3 = ((f32[16,4,8]{2,1,0:T(4,128)}), f32[16,4,8]{2,1,0:T(4,128)S(1)}, u32[]{:S(2)}, u32[]{:S(2)}) async-start(f32[16,4,8]{2,1,0:T(4,128)} %broadcast_in_dim.8), calls=%async_computation.4 | async-start | bytes 65536 | tf_op jit(solution)/shard_map/all_to_all | solution.py:15
  183.4 5.4 %convolution_bitcast_fusion.1 = f32[16,128,256]{2,1,0:T(8,128)} fusion(bf16[16,256,512]{2,1,0:T(8,128)(2,1)} %all-to-all-done.1, bf16[8,16,512]{2,0,1:T(8,128)(2,1)S(1)} %all_to_all.51), kind=kOutput, calls=%fused_computation.11 | convolution fusion | flops 536870912 | bytes 6422528 | tf_op jit(solution)/shard_map/dot_general | solution.py:87
  188.8 5.8 %all-to-all-start.5 = ((f32[16,128,256]{2,1,0:T(8,128)}), f32[16,128,256]{2,1,0:T(8,128)S(1)}, u32[]{:S(2)}, u32[]{:S(2)}) async-start(f32[16,128,256]{2,1,0:T(8,128)} %convolution_bitcast_fusion.1), calls=%async_computation.6 | async-start | bytes 4194304 | tf_op jit(solution)/shard_map/all_to_all | solution.py:41
  194.6 0.7 reshape.64
  195.3 67.5 %all-to-all-done.5 = f32[16,128,256]{2,1,0:T(8,128)S(1)} async-done(((f32[16,128,256]{2,1,0:T(8,128)}), f32[16,128,256]{2,1,0:T(8,128)S(1)}, u32[]{:S(2)}, u32[]{:S(2)}) %all-to-all-start.5) | async-done | bytes 2097184 | tf_op jit(solution)/shard_map/all_to_all | solution.py:41
  262.8 0.8 reduce_sum.48
  263.5 50.0 %reduce-scatter.5.cloned.1.call-done = f32[256,512]{0,1:T(8,128)} async-done(((f32[4096,512]{0,1:T(8,128)}), f32[256,512]{0,1:T(8,128)}) %reduce-scatter.5.cloned.1.call-update) | async-done | bytes 524304 | tf_op jit(solution)/shard_map/reduce_scatter | solution.py:93
  313.6 2.0 copy.17
  (25 shorter events, 0.5 us)
Async XLA Ops:
  7.2 128.7 %copy-start = (bf16[128,4096]{1,0:T(8,128)(2,1)S(1)}, bf16[128,4096]{1,0:T(8,128)(2,1)}, u32[]{:S(2)}) copy-start(bf16[128,4096]{1,0:T(8,128)(2,1)} %param.10) | copy-start | bytes 3145732
  22.3 10.5 %copy-start.2 = (bf16[512]{0:T(512)(128)(2,1)S(1)}, bf16[512]{0:T(512)(128)(2,1)}, u32[]{:S(2)}) copy-start(bf16[512]{0:T(512)(128)(2,1)} %param.8) | copy-start | bytes 3076
  22.3 10.6 %copy-start.1 = (bf16[128,512]{1,0:T(8,128)(2,1)S(1)}, bf16[128,512]{1,0:T(8,128)(2,1)}, u32[]{:S(2)}) copy-start(bf16[128,512]{1,0:T(8,128)(2,1)} %param.7) | copy-start | bytes 393220
  22.3 113.6 %all-to-all-start.1 = ((bf16[16,256,512]{2,1,0:T(8,128)(2,1)}), bf16[16,256,512]{2,1,0:T(8,128)(2,1)}, u32[]{:S(2)}, u32[]{:S(2)}) async-start(bf16[16,256,512]{2,1,0:T(8,128)(2,1)} %stack.2), calls=%async_computation.2 | async-start | bytes 8388608 | tf_op jit(solution)/shard_map/all_to_all | solution.py:57
  32.8 128.0 %reduce-scatter.3.cloned.1.call-start = ((), (), s32[]{:S(2)}) async-start(), calls=%async_computation.8 | async-start | bytes 4456448 | tf_op jit(solution)/shard_map/reduce_scatter | solution.py:65
  39.6 114.9 %copy-start.3 = (s32[2]{0:T(128)S(1)}, s32[2]{0:T(128)}, u32[]{:S(2)}) copy-start(s32[2]{0:T(128)} %param.12) | copy-start | bytes 28
  139.5 20.4 %all-to-all-start.2 = ((f32[16,8,512]{2,1,0:T(8,128)}), f32[16,8,512]{2,1,0:T(8,128)S(1)}, u32[]{:S(2)}, u32[]{:S(2)}) async-start(f32[16,8,512]{2,1,0:T(8,128)} %fusion.10), calls=%async_computation.3 | async-start | bytes 524288 | tf_op jit(solution)/shard_map/all_to_all | solution.py:72
  154.5 159.1 %reduce-scatter.5.cloned.1.call-start = ((), (), s32[]{:S(2)}) async-start(), calls=%async_computation.9 | async-start | bytes 8912896 | tf_op jit(solution)/shard_map/reduce_scatter | solution.py:93
  178.2 10.6 %all-to-all-start.3 = ((f32[16,4,8]{2,1,0:T(4,128)}), f32[16,4,8]{2,1,0:T(4,128)S(1)}, u32[]{:S(2)}, u32[]{:S(2)}) async-start(f32[16,4,8]{2,1,0:T(4,128)} %broadcast_in_dim.8), calls=%async_computation.4 | async-start | bytes 65536 | tf_op jit(solution)/shard_map/all_to_all | solution.py:15
  188.8 74.0 %all-to-all-start.5 = ((f32[16,128,256]{2,1,0:T(8,128)}), f32[16,128,256]{2,1,0:T(8,128)S(1)}, u32[]{:S(2)}, u32[]{:S(2)}) async-start(f32[16,128,256]{2,1,0:T(8,128)} %convolution_bitcast_fusion.1), calls=%async_computation.6 | async-start | bytes 4194304 | tf_op jit(solution)/shard_map/all_to_all | solution.py:41
Sparse Core Ops, SparseCore 0:
  39.7 111.4 reduce-scatter.2
  177.7 135.8 reduce-scatter.4
